TPU v7x, 32 devices: a whole 2x2x4 slice. The times are simulated.
32 devices in a mesh: mesh: 8 (over z, core), run: 4 (over y, x).
Axes of the slice: x: 2, y: 2, z: 4, core: 2. Of those that a mesh axis runs over, the one named last changes fastest.
Arguments:
- snapshots: bfloat16 [16384, 2048], P('mesh', 'run'), may hold values from -6 to 6
- block_cols: int32 [256, 16], P('mesh'), may hold values from 0 to 255, as said below
- mass_blocks: bfloat16 [256, 64, 1024], P('mesh'), as said below
Outputs:
- gram: float32 [2048, 2048], P('mesh', 'run')
Inputs may be any that keep to these rules, and one draw needn't show every extreme that they name: `block_cols`: block row b names 16 different block columns, the first of them b itself; all lie from 2 blocks before the first block row of shard b // 32 to 2 blocks after its last. In every shard but the first, its first block row names the block 2 before the shard; in every shard but the last, its last block row names the block 2 after it. `mass_blocks`: entry [b, i, k * 64 + j] is row i, column j of the k-th stored block of block row b, in the order of block_cols.
All inputs are finite; a program needn't handle non-finite values.
Results may differ from a plain program's by a relative error of at most 0.00056.
Values may be sent and summed in bfloat16 or wider, within the bound.
No kernel may reach another device: no remote copies, remote signals or barrier semaphores. Data moves between devices by JAX's collectives and lax.ppermute only.
A program may use at most 128 MiB of HBM per device.

v0:
```python
import jax
import jax.numpy as jnp
from jax import lax
from jax.sharding import PartitionSpec as P

BLK = 64
HB = 2


def extended(block, sides, width):
    for axis, dim in sides:
        count = lax.axis_size(axis)
        forward = [(i, i + 1) for i in range(count - 1)]
        backward = [(target, source) for source, target in forward]
        low = lax.ppermute(
            lax.slice_in_dim(block, block.shape[dim] - width, None, axis=dim), axis, forward
        )
        high = lax.ppermute(lax.slice_in_dim(block, 0, width, axis=dim), axis, backward)
        block = jnp.concatenate([low, block, high], axis=dim)
    return block


def contract_nodes(left_cols, right_cols):
    return lax.dot_general(
        left_cols, right_cols, (((0,), (0,)), ((), ())), preferred_element_type=jnp.float32
    )


def on_device(snapshots, block_cols, mass_blocks):
    node_count = snapshots.shape[0]
    column_count = snapshots.shape[1]
    blocks_here = node_count // BLK
    stored_count = block_cols.shape[1]
    rim_width = HB * BLK
    padded = extended(snapshots, (("mesh", 0),), rim_width)
    shard_index = lax.axis_index("mesh")
    local_cols = block_cols - (shard_index * blocks_here - HB)
    blocked = padded.reshape(blocks_here + 2 * HB, BLK, column_count)
    picked = blocked[local_cols].reshape(blocks_here, stored_count * BLK, column_count)
    weighted = jnp.einsum("bim,bmc->bic", mass_blocks, picked, preferred_element_type=jnp.float32)
    weighted = weighted.astype(jnp.bfloat16).reshape(node_count, column_count)
    gathered = lax.all_gather(snapshots, "run", axis=1, tiled=True)
    return lax.psum_scatter(
        contract_nodes(gathered, weighted), "mesh", scatter_dimension=0, tiled=True
    )


def solution(mesh):
    placed = (P("mesh", "run"), P("mesh", None), P("mesh", None, None))
    return jax.shard_map(
        on_device, mesh=mesh, in_specs=placed, out_specs=P("mesh", "run"), check_vma=False
    )
```

profile of v0, /device:TPU:0, one launch (start us, length us, event | category | flops | bytes accessed | tf_op | source)
XLA Modules:
  0.0 167.7 jit_solution(6542890312637564476)
XLA Ops:
  6.5 0.0 all-gather.2.cloned.1.call-start
  6.5 0.7 all-gather.2.cloned.1.call-update
  7.3 0.0 reduce-scatter.2.cloned.1.call-start
  7.3 1.0 fusion
  8.3 2.4 %collective-permute-start = (bf16[128,512]{1,0:T(8,128)(2,1)S(1)}, bf16[128,512]{1,0:T(8,128)(2,1)S(1)}, u32[]{:S(2)}, u32[]{:S(2)}) collective-permute-start(bf16[128,512]{1,0:T(8,128)(2,1)S(1)} %get-tuple-element.5), channel_id=1, source_target_pairs={{0,4},{4,8},{8,12},{12,16},{16,20},{20,24},{24,28},{1,5},{5,9},{9,... | collective-permute-start | bytes 393224 | tf_op jit(solution)/shard_map/ppermute | solution.py:15
  10.7 1.3 collective-permute-start.1
  12.0 0.7 compare_select_fusion
  12.7 0.1 copy.5
  12.8 0.1 reshape.14
  12.9 0.0 collective-permute-done
  12.9 3.2 %collective-permute-done.1 = bf16[128,512]{1,0:T(8,128)(2,1)S(1)} collective-permute-done((bf16[128,512]{1,0:T(8,128)(2,1)S(1)}, bf16[128,512]{1,0:T(8,128)(2,1)S(1)}, u32[]{:S(2)}, u32[]{:S(2)}) %collective-permute-start.1) | collective-permute-done | bytes 131104 | tf_op jit(solution)/shard_map/ppermute | solution.py:18
  16.1 1.7 %pad_maximum_fusion = bf16[2304,512]{1,0:T(8,128)(2,1)S(1)} fusion(bf16[128,512]{1,0:T(8,128)(2,1)S(1)} %collective-permute-done.1, bf16[2048,512]{1,0:T(8,128)(2,1)} %param.3, bf16[128,512]{1,0:T(8,128)(2,1)S(1)} %collective-permute-done), kind=kLoop, calls=%fused_computation.2 | loop fusion | flops 7077888 | bytes 4718592 | tf_op jit(solution)/shard_map/concatenate | solution.py:19
  17.9 16.1 %gather_fusion = bf16[512,64,512]{2,1,0:T(8,128)(2,1)} fusion(bf16[36,64,512]{2,1,0:T(8,128)(2,1)S(1)} %bitcast.11, s32[1024]{0:T(1024)S(1)} %pad_clamp_fusion), kind=kCustom, calls=%fused_computation | custom fusion | bytes 67110912 | tf_op jit(solution)/shard_map/gather | solution.py:39
  34.0 17.3 %convolution_convert_fusion = bf16[32,512,64]{1,2,0:T(8,128)(2,1)S(1)} fusion(bf16[32,64,1024]{2,1,0:T(8,128)(2,1)} %param.5, bf16[32,1024,512]{2,1,0:T(8,128)(2,1)} %bitcast.12), kind=kOutput, calls=%fused_computation.3 | convolution fusion | flops 2148532224 | bytes 39845888 | tf_op jit(solution)/shard_map/bim,bmc->bic/dot_general | solution.py:40
  51.2 48.0 %all-gather.2.cloned.1.call-done = bf16[2048,2048]{1,0:T(8,128)(2,1)} async-done(((bf16[2048,512]{1,0:T(8,128)(2,1)}), bf16[2048,2048]{1,0:T(8,128)(2,1)}) %all-gather.2.cloned.1.call-update) | async-done | bytes 8388624 | tf_op jit(solution)/shard_map/all_gather | solution.py:42
  99.3 9.4 %convolution_bitcast_fusion = f32[2048,512]{0,1:T(8,128)} fusion(bf16[2048,512]{1,0:T(8,128)(2,1)S(1)} %bitcast.13, bf16[2048,2048]{1,0:T(8,128)(2,1)} %all-gather.2.cloned.1.call-done), kind=kOutput, calls=%fused_computation.1 | convolution fusion | flops 4294967296 | bytes 14680064 | tf_op jit(solution)/shard_map/dot_general | solution.py:24
  108.7 0.0 reduce-scatter.2.cloned.1.call-update
  108.7 50.1 %reduce-scatter.2.cloned.1.call-done = f32[256,512]{0,1:T(8,128)} async-done(((f32[2048,512]{0,1:T(8,128)}), f32[256,512]{0,1:T(8,128)}) %reduce-scatter.2.cloned.1.call-update) | async-done | bytes 524304 | tf_op jit(solution)/shard_map/reduce_scatter | solution.py:43
  158.8 2.0 %copy.6 = f32[256,512]{1,0:T(8,128)} copy(f32[256,512]{0,1:T(8,128)} %reduce-scatter.2.cloned.1.call-done) | data formatting | bytes 1048576 | tf_op jit(solution)/shard_map/reduce_scatter | solution.py:43
  (1 shorter events, 0.0 us)
Async XLA Ops:
  6.5 92.7 %all-gather.2.cloned.1.call-start = ((), (), s32[]{:S(2)}) async-start(), calls=%async_computation.1 | async-start | bytes 10485760 | tf_op jit(solution)/shard_map/all_gather | solution.py:42
  7.3 151.5 %reduce-scatter.2.cloned.1.call-start = ((), (), s32[]{:S(2)}) async-start(), calls=%async_computation.2 | async-start | bytes 4718592 | tf_op jit(solution)/shard_map/reduce_scatter | solution.py:43
  8.3 4.6 %collective-permute-start = (bf16[128,512]{1,0:T(8,128)(2,1)S(1)}, bf16[128,512]{1,0:T(8,128)(2,1)S(1)}, u32[]{:S(2)}, u32[]{:S(2)}) collective-permute-start(bf16[128,512]{1,0:T(8,128)(2,1)S(1)} %get-tuple-element.5), channel_id=1, source_target_pairs={{0,4},{4,8},{8,12},{12,16},{16,20},{20,24},{24,28},{1,5},{5,9},{9,... | collective-permute-start | bytes 393224 | tf_op jit(solution)/shard_map/ppermute | solution.py:15
  10.7 5.4 %collective-permute-start.1 = (bf16[128,512]{1,0:T(8,128)(2,1)S(1)}, bf16[128,512]{1,0:T(8,128)(2,1)S(1)}, u32[]{:S(2)}, u32[]{:S(2)}) collective-permute-start(bf16[128,512]{1,0:T(8,128)(2,1)S(1)} %get-tuple-element.6), channel_id=1, source_target_pairs={{4,0},{8,4},{12,8},{16,12},{20,16},{24,20},{28,24},{5,1},{9,5},{13... | collective-permute-start | bytes 393224 | tf_op jit(solution)/shard_map/ppermute | solution.py:18
Sparse Core Ops, SparseCore 0:
  9.2 90.0 all-gather.1
  108.8 49.8 reduce-scatter.1
where the time goes:
time: 168 us
  waiting for transfers between devices  102 us (61%)
  matrix products  26.7 us (16%)
  local copies, waits for them, and re-layouts  19.3 us (11%)
  between operations  13.4 us (8%)
  starting transfers between devices  3.74 us (2%)
  other arithmetic  2.46 us (1%)
    reduce_scatter x1, waiting for transfers between devices, on_device(): lax.psum_scatter(contract_nodes(gathered, weighted), 'mesh', scatter_dime...  50.1 us
    all_gather x1, waiting for transfers between devices, on_device(): gathered = lax.all_gather(snapshots, 'run', axis=1, tiled=True)  48 us
    dot_general x1, matrix products, on_device(): jnp.einsum('bim,bmc->bic', mass_blocks, picked, preferred_element_type=jn...  17.3 us
    gather x1, local copies, waits for them, and re-layouts, on_device(): blocked[local_cols].reshape(blocks_here, stored_count * BLK, column_count)  16.1 us
    dot_general x1, matrix products, contract_nodes(): lax.dot_general(left_cols, right_cols, (((0,), (0,)), ((), ())), preferre...  9.44 us
  transfers between devices with their start and end apart: 4, of which 3 were waited for; matrix products, arithmetic and copies ran while one was open for 22% of the time, Pallas kernels for 0%

commit v1 on v0

--- a/solution.py
+++ b/solution.py
@@ -39,7 +39,8 @@
     picked = blocked[local_cols].reshape(blocks_here, stored_count * BLK, column_count)
     weighted = jnp.einsum("bim,bmc->bic", mass_blocks, picked, preferred_element_type=jnp.float32)
     weighted = weighted.astype(jnp.bfloat16).reshape(node_count, column_count)
-    gathered = lax.all_gather(snapshots, "run", axis=1, tiled=True)
+    sent = jnp.stack([snapshots] * lax.axis_size("run"))
+    gathered = jnp.concatenate(lax.all_to_all(sent, "run", 0, 0), axis=1)
     return lax.psum_scatter(
         contract_nodes(gathered, weighted), "mesh", scatter_dimension=0, tiled=True
     )

time: 168 us -> 183 us (1.089)
  local copies, waits for them, and re-layouts: 19.3 us -> 26.5 us
  starting transfers between devices: 3.74 us -> 9.51 us
  waiting for transfers between devices: 102 us -> 104 us
    all_to_all x0 -> x1, waiting for transfers between devices: none -> 49.9 us  [on_device(): gathered = jnp.concatenate(lax.all_to_all(sent, 'run', 0, 0), axis=1)]
    all_gather x1 -> x0, waiting for transfers between devices: 48 us -> none  [on_device(): gathered = lax.all_gather(snapshots, 'run', axis=1, tiled=True)]
    all_to_all x0 -> x1, starting transfers between devices: none -> 5.77 us  [on_device(): gathered = jnp.concatenate(lax.all_to_all(sent, 'run', 0, 0), axis=1)]
    another operation x0 -> x1, local copies, waits for them, and re-layouts: none -> 4.26 us  [on_device(): sent = jnp.stack([snapshots] * lax.axis_size('run'))]
    unnamed x0 -> x3, local copies, waits for them, and re-layouts: none -> 2.93 us
  transfers between devices with their start and end apart: 4 -> 4, of which waited for: 3 -> 3; matrix products, arithmetic and copies ran while one was open for 22% -> 20% of each run, Pallas kernels for 0% -> 0%
where the time goes in v1:
time: 183 us; the launch traced here: 182 us
  waiting for transfers between devices  104 us (57%)
  matrix products  26.9 us (15%)
  local copies, waits for them, and re-layouts  26.5 us (14%)
  between operations  13.5 us (7%)
  starting transfers between devices  9.51 us (5%)
    reduce_scatter x1, waiting for transfers between devices, on_device(): lax.psum_scatter(contract_nodes(gathered, weighted), 'mesh', scatter_dime...  50.6 us
    all_to_all x1, waiting for transfers between devices, on_device(): gathered = jnp.concatenate(lax.all_to_all(sent, 'run', 0, 0), axis=1)  49.9 us
    dot_general x1, matrix products, on_device(): jnp.einsum('bim,bmc->bic', mass_blocks, picked, preferred_element_type=jn...  17.3 us
    gather x1, local copies, waits for them, and re-layouts, on_device(): blocked[local_cols].reshape(blocks_here, stored_count * BLK, column_count)  16.1 us
    dot_general x1, matrix products, contract_nodes(): lax.dot_general(left_cols, right_cols, (((0,), (0,)), ((), ())), preferre...  9.62 us
    all_to_all x1, starting transfers between devices, on_device(): gathered = jnp.concatenate(lax.all_to_all(sent, 'run', 0, 0), axis=1)  5.77 us
    another operation x1, local copies, waits for them, and re-layouts, on_device(): sent = jnp.stack([snapshots] * lax.axis_size('run'))  4.26 us
    ppermute x1, waiting for transfers between devices, extended(): lax.ppermute(lax.slice_in_dim(block, 0, width, axis=dim), axis, backward)  3.91 us
  transfers between devices with their start and end apart: 4, of which 3 were waited for; matrix products, arithmetic and copies ran while one was open for 20% of the time, Pallas kernels for 0%

profile of v1, /device:TPU:0, one launch (start us, length us, event | category | flops | bytes accessed | tf_op | source)
XLA Modules:
  0.0 182.5 jit_solution(2643853402996531500)
XLA Ops:
  6.5 2.9 %copy.6 = bf16[2048,512]{0,1:T(8,128)(2,1)S(1)} copy(bf16[2048,512]{1,0:T(8,128)(2,1)} %param.3) | data formatting | bytes 4194304 | tf_op args[0]
  9.5 4.3 %stack.2 = bf16[4,2048,512]{1,2,0:T(8,128)(2,1)} broadcast(bf16[2048,512]{0,1:T(8,128)(2,1)S(1)} %copy.6), dimensions={1,2} | broadcast | bytes 10485760 | tf_op jit(solution)/shard_map/stack | solution.py:42
  13.7 0.0 copy-start
  13.7 5.8 %all-to-all-start = ((bf16[4,2048,512]{1,2,0:T(8,128)(2,1)}), bf16[4,2048,512]{1,2,0:T(8,128)(2,1)}, u32[]{:S(2)}, u32[]{:S(2)}) async-start(bf16[4,2048,512]{1,2,0:T(8,128)(2,1)} %stack.2), calls=%async_computation | async-start | bytes 16777216 | tf_op jit(solution)/shard_map/all_to_all | solution.py:43
  19.5 0.0 reduce-scatter.2.cloned.1.call-start
  19.6 1.0 fusion
  20.6 2.4 %collective-permute-start = (bf16[128,512]{1,0:T(8,128)(2,1)S(1)}, bf16[128,512]{1,0:T(8,128)(2,1)S(1)}, u32[]{:S(2)}, u32[]{:S(2)}) collective-permute-start(bf16[128,512]{1,0:T(8,128)(2,1)S(1)} %get-tuple-element.5), channel_id=1, source_target_pairs={{0,4},{4,8},{8,12},{12,16},{16,20},{20,24},{24,28},{1,5},{5,9},{9,... | collective-permute-start | bytes 393224 | tf_op jit(solution)/shard_map/ppermute | solution.py:15
  23.0 1.3 collective-permute-start.1
  24.3 0.0 copy-done
  24.3 0.1 copy.5
  24.4 0.1 reshape.24
  24.5 0.0 collective-permute-done
  24.5 3.9 %collective-permute-done.1 = bf16[128,512]{1,0:T(8,128)(2,1)S(1)} collective-permute-done((bf16[128,512]{1,0:T(8,128)(2,1)S(1)}, bf16[128,512]{1,0:T(8,128)(2,1)S(1)}, u32[]{:S(2)}, u32[]{:S(2)}) %collective-permute-start.1) | collective-permute-done | bytes 131104 | tf_op jit(solution)/shard_map/ppermute | solution.py:18
  28.4 1.7 pad_maximum_fusion
  30.1 16.1 %gather_fusion = bf16[512,64,512]{2,1,0:T(8,128)(2,1)} fusion(bf16[36,64,512]{2,1,0:T(8,128)(2,1)S(1)} %bitcast.14, s32[1024]{0:T(1024)S(1)} %pad_clamp_fusion), kind=kCustom, calls=%fused_computation | custom fusion | bytes 67110912 | tf_op jit(solution)/shard_map/gather | solution.py:39
  46.2 17.3 %convolution_convert_fusion = bf16[32,512,64]{1,2,0:T(8,128)(2,1)S(1)} fusion(bf16[32,64,1024]{2,1,0:T(8,128)(2,1)} %param.5, bf16[32,1024,512]{2,1,0:T(8,128)(2,1)} %bitcast.15), kind=kOutput, calls=%fused_computation.3 | convolution fusion | flops 2148532224 | bytes 39845888 | tf_op jit(solution)/shard_map/bim,bmc->bic/dot_general | solution.py:40
  63.5 49.9 %all-to-all-done = bf16[4,2048,512]{1,2,0:T(8,128)(2,1)} async-done(((bf16[4,2048,512]{1,2,0:T(8,128)(2,1)}), bf16[4,2048,512]{1,2,0:T(8,128)(2,1)}, u32[]{:S(2)}, u32[]{:S(2)}) %all-to-all-start) | async-done | bytes 8388640 | tf_op jit(solution)/shard_map/all_to_all | solution.py:43
  113.4 9.6 %convolution_bitcast_fusion = f32[2048,512]{0,1:T(8,128)} fusion(bf16[2048,512]{1,0:T(8,128)(2,1)S(1)} %bitcast.16, bf16[2048,2048]{0,1:T(8,128)(2,1)} %bitcast.5), kind=kOutput, calls=%fused_computation.1 | convolution fusion | flops 4294967296 | bytes 14680064 | tf_op jit(solution)/shard_map/dot_general | solution.py:24
  123.0 0.0 reduce-scatter.2.cloned.1.call-update
  123.0 50.6 %reduce-scatter.2.cloned.1.call-done = f32[256,512]{0,1:T(8,128)} async-done(((f32[2048,512]{0,1:T(8,128)}), f32[256,512]{0,1:T(8,128)}) %reduce-scatter.2.cloned.1.call-update) | async-done | bytes 524304 | tf_op jit(solution)/shard_map/reduce_scatter | solution.py:44
  173.6 2.0 %copy.7 = f32[256,512]{1,0:T(8,128)} copy(f32[256,512]{0,1:T(8,128)} %reduce-scatter.2.cloned.1.call-done) | data formatting | bytes 1048576 | tf_op jit(solution)/shard_map/reduce_scatter | solution.py:44
  (2 shorter events, 0.0 us)
Async XLA Ops:
  13.7 10.5 %copy-start = (s32[32,16]{0,1:T(8,128)S(1)}, s32[32,16]{0,1:T(8,128)}, u32[]{:S(2)}) copy-start(s32[32,16]{0,1:T(8,128)} %param.4) | copy-start | bytes 6148
  13.7 99.7 %all-to-all-start = ((bf16[4,2048,512]{1,2,0:T(8,128)(2,1)}), bf16[4,2048,512]{1,2,0:T(8,128)(2,1)}, u32[]{:S(2)}, u32[]{:S(2)}) async-start(bf16[4,2048,512]{1,2,0:T(8,128)(2,1)} %stack.2), calls=%async_computation | async-start | bytes 16777216 | tf_op jit(solution)/shard_map/all_to_all | solution.py:43
  19.5 154.1 %reduce-scatter.2.cloned.1.call-start = ((), (), s32[]{:S(2)}) async-start(), calls=%async_computation.2 | async-start | bytes 4718592 | tf_op jit(solution)/shard_map/reduce_scatter | solution.py:44
  20.6 3.9 %collective-permute-start = (bf16[128,512]{1,0:T(8,128)(2,1)S(1)}, bf16[128,512]{1,0:T(8,128)(2,1)S(1)}, u32[]{:S(2)}, u32[]{:S(2)}) collective-permute-start(bf16[128,512]{1,0:T(8,128)(2,1)S(1)} %get-tuple-element.5), channel_id=1, source_target_pairs={{0,4},{4,8},{8,12},{12,16},{16,20},{20,24},{24,28},{1,5},{5,9},{9,... | collective-permute-start | bytes 393224 | tf_op jit(solution)/shard_map/ppermute | solution.py:15
  23.0 5.4 %collective-permute-start.1 = (bf16[128,512]{1,0:T(8,128)(2,1)S(1)}, bf16[128,512]{1,0:T(8,128)(2,1)S(1)}, u32[]{:S(2)}, u32[]{:S(2)}) collective-permute-start(bf16[128,512]{1,0:T(8,128)(2,1)S(1)} %get-tuple-element.6), channel_id=1, source_target_pairs={{4,0},{8,4},{12,8},{16,12},{20,16},{24,20},{28,24},{5,1},{9,5},{13... | collective-permute-start | bytes 393224 | tf_op jit(solution)/shard_map/ppermute | solution.py:18
Sparse Core Ops, SparseCore 0:
  123.2 50.3 reduce-scatter.1
